TPU v7x, 256 devices: a whole 4x4x8 slice. The times are simulated.
256 devices in a mesh: side: 2 (over y_hi), row: 8 (over z), col: 16 (over x, y_lo, core).
Axes of the slice: x: 4, y: 4 (y_hi: 2, y_lo: 2; y = y_hi * 2 + y_lo), z: 8, core: 2. Of those that a mesh axis runs over, the one named last changes fastest.
Arguments:
- queries: bfloat16 [512, 8192], P(('row', 'col')), may hold values from -4.5 to 16
- new_entries: bfloat16 [512, 2048], P(('row', 'col')), may hold values from -4.5 to 15.875
- cache_keys: bfloat16 [2, 512, 256, 1024], P('side', ('row', 'col')), may hold values from -4.5 to 16
- cache_values: bfloat16 [2, 512, 256, 1024], P('side', ('row', 'col')), may hold values from -6 to 6
- lengths: int32 [512], P(('row', 'col')), may hold values from 1 to 256, 32768 in all
- residual: bfloat16 [512, 8192], P(None, 'col'), may hold values from -16 to 16
- norm_gain: bfloat16 [8192], P('col'), may hold values from 0.099609375 to 1.8984375
- out_weight: bfloat16 [2, 8192, 8192], P('side', 'row', 'col'), may hold values from -0.125 to 0.125
- gate_weight: bfloat16 [2, 8192, 14336], P('side', 'col', 'row'), may hold values from -0.0625 to 0.0625
- up_weight: bfloat16 [2, 8192, 14336], P('side', 'col', 'row'), may hold values from -0.0625 to 0.0625
- down_weight: bfloat16 [2, 14336, 8192], P('side', 'row', 'col'), may hold values from -0.046875 to 0.046875
Outputs:
- layer_out: bfloat16 [512, 8192], P(('row', 'col'), 'side')
All inputs are finite; a program needn't handle non-finite values. No bound on the sum of `lengths` on one device may be relied on, other than what follows from the above.
Results may differ from a plain program's by a relative error of at most 0.025.
Values may be sent and summed in bfloat16 or wider, within the bound.
No kernel may reach another device: no remote copies, remote signals or barrier semaphores. Data moves between devices by JAX's collectives and lax.ppermute only.
A program may use at most 64 MiB of HBM per device.

v0:
```python
import jax
import jax.numpy as jnp
from jax import lax
from jax.sharding import PartitionSpec as P

D = 8192
H = 64
KVH = 8
HD = 128
ORIG = 64
rope_theta = 500000.0
stretch_factor = 8.0
eps = 1e-05


def from_behind(value, axis, steps):
    count = lax.axis_size(axis)
    first, last = (max(0, -steps), min(count, count - steps))
    return lax.ppermute(value, axis, [(source, source + steps) for source in range(first, last)])


def frequencies(lengths):
    seq = lengths.astype(jnp.float32) + 1.0
    stretch = jnp.maximum(stretch_factor * seq / ORIG - (stretch_factor - 1.0), 1.0)
    log_base = jnp.log(jnp.float32(rope_theta)) + HD / (HD - 2.0) * jnp.log(stretch)
    expo = jnp.arange(HD // 2).astype(jnp.float32) * (2.0 / HD)
    return jnp.exp(-expo[None, :] * log_base[:, None])


def rotary(vec, angles):
    half = vec.shape[-1] // 2
    first = vec[..., :half]
    second = vec[..., half:]
    cosine = jnp.cos(angles)
    sine = jnp.sin(angles)
    return jnp.concatenate(
        [first * cosine - second * sine, second * cosine + first * sine], axis=-1
    )


def attention(queries, new_entries, keys, values, lengths):
    slots = queries.shape[0]
    span = keys.shape[1]
    per_group = H // KVH
    freqs = frequencies(lengths)
    angle_new = lengths.astype(jnp.float32)[:, None] * freqs
    angle_cache = jnp.arange(span).astype(jnp.float32)[None, :, None] * freqs[:, None, :]
    query_rot = rotary(
        queries.astype(jnp.float32).reshape(slots, H, HD), angle_new[:, None, :]
    ).astype(jnp.bfloat16)
    query_rot = query_rot.reshape(slots, KVH, per_group, HD)
    key_fresh = new_entries[:, : KVH * HD].astype(jnp.float32).reshape(slots, KVH, HD)
    value_fresh = new_entries[:, KVH * HD :].astype(jnp.float32).reshape(slots, KVH, HD)
    key_new_rot = rotary(key_fresh, angle_new[:, None, :]).astype(jnp.bfloat16)
    key_rot = rotary(
        keys.astype(jnp.float32).reshape(slots, span, KVH, HD), angle_cache[:, :, None, :]
    ).astype(jnp.bfloat16)
    scale = HD ** (-0.5)
    scores = (
        jnp.einsum("sgqd,scgd->sgqc", query_rot, key_rot, preferred_element_type=jnp.float32)
        * scale
    )
    own_score = (
        jnp.einsum("sgqd,sgd->sgq", query_rot, key_new_rot, preferred_element_type=jnp.float32)
        * scale
    )
    valid_mask = (jnp.arange(span)[None, :] < lengths[:, None])[:, None, None, :]
    highest = jnp.maximum(jnp.max(jnp.where(valid_mask, scores, -1e30), axis=-1), own_score)
    weights = jnp.where(valid_mask, jnp.exp(scores - highest[..., None]), 0.0)
    own_weight = jnp.exp(own_score - highest)
    totals = jnp.sum(weights, axis=-1) + own_weight
    weights16 = weights.astype(jnp.bfloat16)
    mixed = jnp.einsum(
        "sgqc,scgd->sgqd",
        weights16,
        values.reshape(slots, span, KVH, HD),
        preferred_element_type=jnp.float32,
    )
    mixed = mixed + own_weight[..., None] * value_fresh[:, :, None, :]
    return (mixed / totals[..., None]).reshape(slots, H * HD).astype(jnp.bfloat16)


def local(
    queries,
    new_entries,
    cache_keys,
    cache_values,
    lengths,
    residual,
    norm_gain,
    out_weight,
    gate_weight,
    up_weight,
    down_weight,
):
    attended = attention(queries, new_entries, cache_keys[0], cache_values[0], lengths)
    slot_count = attended.shape[0]
    row_count = lax.axis_size("row")
    col_count = lax.axis_size("col")
    head_block = attended.shape[1] // row_count
    split_heads = attended.reshape(slot_count, row_count, head_block)
    moved = from_behind(split_heads, "side", 1)
    blocks = lax.all_to_all(moved, "row", split_axis=1, concat_axis=0, tiled=True)
    sectioned = blocks.reshape(row_count, 1, slot_count, head_block)
    out_block = out_weight[0]
    partial_value = jnp.einsum(
        "akjd,de->akje",
        lax.all_gather(sectioned, "col", axis=1, tiled=True),
        out_block,
        preferred_element_type=jnp.float32,
    )
    col_width = out_block.shape[1]
    total_rows = row_count * col_count * slot_count
    projected = lax.psum(
        partial_value.reshape(total_rows, col_width).astype(jnp.bfloat16), "row"
    ).astype(jnp.float32)
    stream = residual.astype(jnp.float32) + projected
    squares = lax.psum(jnp.sum(stream * stream, axis=1), "col")
    inv_rms = lax.rsqrt(squares / D + eps)
    normed = (stream * inv_rms[:, None] * norm_gain.astype(jnp.float32)[None, :]).astype(
        jnp.bfloat16
    )
    gate_block = gate_weight[0]
    up_block = up_weight[0]
    down_block = down_weight[0]
    gate_part = jnp.dot(normed, gate_block, preferred_element_type=jnp.float32)
    up_part = jnp.dot(normed, up_block, preferred_element_type=jnp.float32)
    gate_total, up_total = (
        lax.psum(gate_part.astype(jnp.bfloat16), "col").astype(jnp.float32),
        lax.psum(up_part.astype(jnp.bfloat16), "col").astype(jnp.float32),
    )
    hidden = (jax.nn.silu(gate_total) * up_total).astype(jnp.bfloat16)
    down_part = jnp.dot(hidden, down_block, preferred_element_type=jnp.float32)
    down_total = lax.psum(down_part.astype(jnp.bfloat16), "row").astype(jnp.float32)
    final = (stream + down_total).astype(jnp.bfloat16)
    group_rows = col_count * slot_count
    mine_rows = lax.dynamic_slice_in_dim(final, lax.axis_index("row") * group_rows, group_rows, 0)
    slot_rows = lax.all_to_all(mine_rows, "col", split_axis=0, concat_axis=1, tiled=True)
    half_width = slot_rows.shape[1] // 2
    returned = from_behind(slot_rows[:, :half_width], "side", -1)
    return jnp.where(lax.axis_index("side") == 0, returned, slot_rows[:, half_width:])


def solution(mesh):
    in_specs = (
        P(("row", "col"), None),
        P(("row", "col"), None),
        P("side", ("row", "col"), None, None),
        P("side", ("row", "col"), None, None),
        P(("row", "col")),
        P(None, "col"),
        P("col"),
        P("side", "row", "col"),
        P("side", "col", "row"),
        P("side", "col", "row"),
        P("side", "row", "col"),
    )
    out_specs = P(("row", "col"), "side")
    return jax.shard_map(local, mesh=mesh, in_specs=in_specs, out_specs=out_specs, check_vma=False)
```

profile of v0, /device:TPU:1, one launch (start us, length us, event | category | flops | bytes accessed | tf_op | source)
XLA Modules:
  0.0 439.4 jit_solution(3323142169381161737)
XLA Ops:
  6.5 0.0 copy-start
  6.5 0.0 all-gather.3.cloned.1.call-start
  6.5 0.8 convert_element_type.82
  7.3 0.7 multiply_add_fusion
  8.0 0.7 iota_compare_fusion
  8.7 3.9 copy.23
  12.7 4.2 fusion.50
  16.8 3.8 copy.32
  20.6 0.0 copy-start.4
  20.6 0.0 copy-start.5
  20.6 3.8 copy.33
  24.5 0.0 copy-done.4
  24.5 0.0 copy-done.5
  24.5 0.1 multiply_cosine_fusion.1
  24.7 0.1 fusion.41
  24.8 0.1 subtract_convert_fusion.2
  24.9 1.9 multiply_cosine_fusion
  26.7 0.1 maximum_bitcast_fusion
  26.8 0.2 fusion.43
  27.1 4.7 %subtract_convert_fusion = (bf16[4,256,8,64]{3,1,2,0:T(8,128)(2,1)S(1)}, bf16[4,256,8,64]{3,1,2,0:T(8,128)(2,1)S(1)}) fusion(f32[4,256,8,64]{3,1,2,0:T(8,128)} %copy.33, f32[4,256,8,64]{3,1,2,0:T(8,128)} %copy.32, f32[4,256,64]{2,1,0:T(8,128)S(1)} %get-tuple-element.22, f32[4,256,64]{2,1,0:T(8,128)S(1)} %get-tuple-element.21), kind=kLoop, calls=%fused_computation.3 | loop fusion | flops 4194304 | bytes 6815744 | tf_op jit(solution)/shard_map/convert.6
  31.8 0.0 copy-start.1
  31.8 1.3 select_reduce_fusion
  33.2 0.2 fusion.34
  33.4 0.0 copy-done.1
  33.4 0.6 copy.36
  34.0 0.4 fusion.30
  34.5 0.1 copy.27
  34.6 5.7 %collective-permute-start = (bf16[4,8,1024]{2,0,1:T(4,128)(2,1)S(1)}, bf16[4,8,1024]{2,0,1:T(4,128)(2,1)S(1)}, u32[]{:S(2)}, u32[]{:S(2)}) collective-permute-start(bf16[4,8,1024]{2,0,1:T(4,128)(2,1)S(1)} %copy.27), channel_id=1, source_target_pairs={{0,128},{1,129},{2,130},{3,131},{4,132},{5,133},{6,134},{7,135},{8... | collective-permute-start | bytes 196616 | tf_op jit(solution)/shard_map/ppermute | solution.py:19
  40.3 1.3 collective-permute-done
  41.6 15.3 %all_to_all.34 = bf16[4,8,1024]{2,0,1:T(4,128)(2,1)S(1)} all-to-all(bf16[4,8,1024]{2,0,1:T(4,128)(2,1)S(1)} %collective-permute-done), channel_id=1, replica_groups=mesh['side'=2,'row'=8,'col'=16] {'row'}, dimensions={1} | all-to-all | bytes 131072 | tf_op jit(solution)/shard_map/all_to_all | solution.py:103
  56.9 0.6 copy.28
  57.5 0.0 all-gather.3.cloned.1.call-update
  57.5 0.0 all-reduce.5.cloned.1.call-start
  57.6 34.6 %all-gather.3.cloned.1.call-done = bf16[8,64,1,1024]{3,0,2,1:T(8,128)(2,1)} async-done(((bf16[8,4,1,1024]{3,0,2,1:T(8,128)(2,1)}), bf16[8,64,1,1024]{3,0,2,1:T(8,128)(2,1)}) %all-gather.3.cloned.1.call-update) | async-done | bytes 1048592 | tf_op jit(solution)/shard_map/all_gather | solution.py:108
  92.2 1.8 copy.29
  94.0 0.0 copy-start.6
  94.0 0.0 copy-start.2
  94.1 2.8 convolution_convert_fusion.2
  96.9 0.0 all-reduce.5.cloned.1.call-update
  96.9 0.0 all-reduce.9.cloned.1.call-start
  96.9 0.0 copy-done.6
  96.9 68.6 %all-reduce.5.cloned.1.call-done = bf16[512,512]{1,0:T(8,128)(2,1)} async-done(((bf16[512,512]{1,0:T(8,128)(2,1)}), bf16[512,512]{1,0:T(8,128)(2,1)}) %all-reduce.5.cloned.1.call-update) | async-done | bytes 524304 | tf_op jit(solution)/shard_map/psum | solution.py:114
  165.5 0.0 copy-done.2
  165.5 1.3 multiply_reduce_fusion
  166.8 31.7 %psum.36 = f32[512]{0:T(512)S(1)} all-reduce(f32[512]{0:T(512)S(1)} %get-tuple-element.13), channel_id=1, replica_groups=mesh['side'=2,'row'=8,'col'=16] {'col'}, use_global_device_ids=true, to_apply=%region_4.5 | all-reduce | flops 512 | bytes 4096 | tf_op jit(solution)/shard_map/psum | solution.py:118
  198.6 0.0 copy-done
  198.6 0.0 copy-start.3
  198.6 0.0 copy-start.7
  198.6 3.6 convolution_convert_fusion.1
  202.2 0.0 copy-done.3
  202.2 0.0 copy-done.7
  202.2 2.5 convolution_convert_fusion
  204.7 0.0 all-reduce.9.cloned.1.call-update
  204.7 0.0 all-reduce.7.cloned.1.call-start
  204.8 129.6 %all-reduce.9.cloned.1.call-done = (bf16[512,1792]{1,0:T(8,128)(2,1)}, bf16[512,1792]{1,0:T(8,128)(2,1)}) async-done(((bf16[512,1792]{1,0:T(8,128)(2,1)}, bf16[512,1792]{1,0:T(8,128)(2,1)}), (bf16[512,1792]{1,0:T(8,128)(2,1)}, bf16[512,1792]{1,0:T(8,128)(2,1)})) %all-reduce.9.cloned.1.call-update) | async-done | bytes 3670032 | tf_op jit(solution)/shard_map/psum | solution.py:130
  334.4 4.6 %fusion.16 = bf16[512,512]{1,0:T(8,128)(2,1)} fusion(bf16[1,1792,512]{2,1,0:T(8,128)(2,1)} %param.21, bf16[512,1792]{1,0:T(8,128)(2,1)} %get-tuple-element.5, bf16[512,1792]{1,0:T(8,128)(2,1)} %get-tuple-element.6), kind=kOutput, calls=%fused_computation.21 | convolution fusion | flops 947126272 | bytes 6029312 | tf_op jit(solution)/shard_map/dot_general | solution.py:133
  339.0 0.0 all-reduce.7.cloned.1.call-update
  339.0 70.0 %all-reduce.7.cloned.1.call-done = bf16[512,512]{1,0:T(8,128)(2,1)} async-done(((bf16[512,512]{1,0:T(8,128)(2,1)}), bf16[512,512]{1,0:T(8,128)(2,1)}) %all-reduce.7.cloned.1.call-update) | async-done | bytes 524304 | tf_op jit(solution)/shard_map/psum | solution.py:134
  409.1 0.9 fusion.37
  409.9 16.1 %all_to_all.35 = bf16[16,4,512]{2,1,0:T(4,128)(2,1)S(1)} all-to-all(bf16[16,4,512]{2,1,0:T(4,128)(2,1)S(1)} %all_to_all.28), channel_id=1, replica_groups=mesh['side'=2,'row'=8,'col'=16] {'col'}, dimensions={0} | all-to-all | bytes 131072 | tf_op jit(solution)/shard_map/all_to_all | solution.py:138
  426.0 1.3 collective-permute-start.1
  427.3 4.9 %collective-permute-done.1 = bf16[4,4096]{1,0:T(4,128)(2,1)S(1)} collective-permute-done((bf16[4,4096]{1,0:T(4,128)(2,1)S(1)}, bf16[4,4096]{1,0:T(4,128)(2,1)S(1)}, u32[]{:S(2)}, u32[]{:S(2)}) %collective-permute-start.1) | collective-permute-done | bytes 32800 | tf_op jit(solution)/shard_map/ppermute | solution.py:19
  432.2 0.6 slice_select_fusion
  (13 shorter events, 0.2 us)
Async XLA Ops:
  6.5 192.0 %copy-start = (bf16[1,512,1792]{2,1,0:T(8,128)(2,1)S(1)}, bf16[1,512,1792]{2,1,0:T(8,128)(2,1)}, u32[]{:S(2)}) copy-start(bf16[1,512,1792]{2,1,0:T(8,128)(2,1)} %param.19) | copy-start | bytes 5505028
  6.5 85.7 %all-gather.3.cloned.1.call-start = ((), (), s32[]{:S(2)}) async-start(), calls=%async_computation.4 | async-start | bytes 1114112 | tf_op jit(solution)/shard_map/all_gather | solution.py:108
  20.6 3.8 copy-start.4
  20.6 3.9 copy-start.5
  31.8 1.6 copy-start.1
  34.6 7.0 %collective-permute-start = (bf16[4,8,1024]{2,0,1:T(4,128)(2,1)S(1)}, bf16[4,8,1024]{2,0,1:T(4,128)(2,1)S(1)}, u32[]{:S(2)}, u32[]{:S(2)}) collective-permute-start(bf16[4,8,1024]{2,0,1:T(4,128)(2,1)S(1)} %copy.27), channel_id=1, source_target_pairs={{0,128},{1,129},{2,130},{3,131},{4,132},{5,133},{6,134},{7,135},{8... | collective-permute-start | bytes 196616 | tf_op jit(solution)/shard_map/ppermute | solution.py:19
  57.5 108.0 %all-reduce.5.cloned.1.call-start = ((), (), s32[]{:S(2)}) async-start(), calls=%async_computation.2 | async-start | bytes 1048576 | tf_op jit(solution)/shard_map/psum | solution.py:114
  94.0 2.9 copy-start.6
  94.0 71.5 %copy-start.2 = (bf16[512,512]{1,0:T(8,128)(2,1)S(1)}, bf16[512,512]{1,0:T(8,128)(2,1)}, u32[]{:S(2)}) copy-start(bf16[512,512]{1,0:T(8,128)(2,1)} %param.16) | copy-start | bytes 1572868
  96.9 237.5 %all-reduce.9.cloned.1.call-start = ((), (), s32[]{:S(2)}) async-start(), calls=%async_computation.5 | async-start | bytes 7340032 | tf_op jit(solution)/shard_map/psum | solution.py:130
  198.6 3.7 copy-start.3
  198.6 3.7 copy-start.7
  204.7 204.3 %all-reduce.7.cloned.1.call-start = ((), (), s32[]{:S(2)}) async-start(), calls=%async_computation.3 | async-start | bytes 1048576 | tf_op jit(solution)/shard_map/psum | solution.py:134
  426.0 6.2 %collective-permute-start.1 = (bf16[4,4096]{1,0:T(4,128)(2,1)S(1)}, bf16[4,4096]{1,0:T(4,128)(2,1)S(1)}, u32[]{:S(2)}, u32[]{:S(2)}) collective-permute-start(bf16[4,4096]{1,0:T(4,128)(2,1)S(1)} %slice.46), channel_id=1, source_target_pairs={{128,0},{129,1},{130,2},{131,3},{132,4},{133,5},{134,6},{135,7},{1... | collective-permute-start | bytes 98312 | tf_op jit(solution)/shard_map/ppermute | solution.py:19
Sparse Core Ops, SparseCore 0:
  57.7 34.5 all-gather.2
  97.0 68.4 all-reduce.4
  204.8 129.5 all-reduce.8
  339.1 69.8 all-reduce.6
where the time goes:
time: 440 us; the launch traced here: 439 us
  waiting for transfers between devices  309 us (70%)
  blocking collectives  63.1 us (14%)
  local copies, waits for them, and re-layouts  19 us (4%)
  matrix products  15.5 us (4%)
  between operations  13.3 us (3%)
  other arithmetic  12.2 us (3%)
  starting transfers between devices  7.07 us (2%)
    psum x1, waiting for transfers between devices, local(): lax.psum(up_part.astype(jnp.bfloat16), 'col').astype(jnp.float32)  130 us
    psum x1, waiting for transfers between devices, local(): lax.psum(down_part.astype(jnp.bfloat16), 'row').astype(jnp.float32)  70 us
    psum x1, waiting for transfers between devices, local(): lax.psum(partial_value.reshape(total_rows, col_width).astype(jnp.bfloat16...  68.6 us
    all_gather x1, waiting for transfers between devices, local(): lax.all_gather(sectioned, 'col', axis=1, tiled=True)  34.6 us
    psum x1, blocking collectives, local(): squares = lax.psum(jnp.sum(stream * stream, axis=1), 'col')  31.7 us
    all_to_all x1, blocking collectives, local(): lax.all_to_all(mine_rows, 'col', split_axis=0, concat_axis=1, tiled=True)  16.1 us
    all_to_all x1, blocking collectives, local(): lax.all_to_all(moved, 'row', split_axis=1, concat_axis=0, tiled=True)  15.3 us
    unnamed x21, local copies, waits for them, and re-layouts  12.2 us
  transfers between devices with their start and end apart: 6, of which 6 were waited for; matrix products, arithmetic and copies ran while one was open for 0% of the time, Pallas kernels for 0%

commit v1 on v0

--- a/solution.py
+++ b/solution.py
@@ -135,7 +135,12 @@
     final = (stream + down_total).astype(jnp.bfloat16)
     group_rows = col_count * slot_count
     mine_rows = lax.dynamic_slice_in_dim(final, lax.axis_index("row") * group_rows, group_rows, 0)
-    slot_rows = lax.all_to_all(mine_rows, "col", split_axis=0, concat_axis=1, tiled=True)
+    slot_rows = jnp.concatenate(
+        jax.lax.all_to_all(
+            jnp.stack(jnp.split(mine_rows, jax.lax.axis_size("col"), 0)), "col", 0, 0
+        ),
+        axis=1,
+    )
     half_width = slot_rows.shape[1] // 2
     returned = from_behind(slot_rows[:, :half_width], "side", -1)
     return jnp.where(lax.axis_index("side") == 0, returned, slot_rows[:, half_width:])

time: 440 us -> 440 us (level)
    unnamed x21 -> x36, local copies, waits for them, and re-layouts: 12.2 us -> 12.4 us
where the time goes in v1:
time: 440 us
  waiting for transfers between devices  309 us (70%)
  blocking collectives  63.1 us (14%)
  local copies, waits for them, and re-layouts  19.1 us (4%)
  matrix products  15.5 us (4%)
  between operations  13.4 us (3%)
  other arithmetic  12.2 us (3%)
  starting transfers between devices  7.07 us (2%)
    psum x1, waiting for transfers between devices, local(): lax.psum(up_part.astype(jnp.bfloat16), 'col').astype(jnp.float32)  130 us
    psum x1, waiting for transfers between devices, local(): lax.psum(down_part.astype(jnp.bfloat16), 'row').astype(jnp.float32)  70 us
    psum x1, waiting for transfers between devices, local(): lax.psum(partial_value.reshape(total_rows, col_width).astype(jnp.bfloat16...  68.6 us
    all_gather x1, waiting for transfers between devices, local(): lax.all_gather(sectioned, 'col', axis=1, tiled=True)  34.6 us
    psum x1, blocking collectives, local(): squares = lax.psum(jnp.sum(stream * stream, axis=1), 'col')  31.7 us
    all_to_all x1, blocking collectives, local(): jax.lax.all_to_all(jnp.stack(jnp.split(mine_rows, jax.lax.axis_size('col'...  16.1 us
    all_to_all x1, blocking collectives, local(): lax.all_to_all(moved, 'row', split_axis=1, concat_axis=0, tiled=True)  15.3 us
    unnamed x36, local copies, waits for them, and re-layouts  12.4 us
  transfers between devices with their start and end apart: 6, of which 6 were waited for; matrix products, arithmetic and copies ran while one was open for 0% of the time, Pallas kernels for 0%

profile of v1, /device:TPU:1, one launch (start us, length us, event | category | flops | bytes accessed | tf_op | source)
XLA Modules:
  0.0 439.6 jit_solution(7047048930196050104)
XLA Ops:
  6.5 0.0 copy-start
  6.5 0.0 all-gather.3.cloned.1.call-start
  6.5 0.8 convert_element_type.82
  7.3 0.7 multiply_add_fusion
  8.0 0.7 iota_compare_fusion
  8.7 3.9 copy.23
  12.7 4.2 fusion.50
  16.8 3.8 copy.32
  20.6 0.0 copy-start.4
  20.6 0.0 copy-start.5
  20.6 3.8 copy.33
  24.5 0.0 copy-done.4
  24.5 0.0 copy-done.5
  24.5 0.1 multiply_cosine_fusion.1
  24.7 0.1 fusion.41
  24.8 0.1 subtract_convert_fusion.2
  24.9 1.9 multiply_cosine_fusion
  26.7 0.1 maximum_bitcast_fusion
  26.8 0.2 fusion.43
  27.1 4.7 %subtract_convert_fusion = (bf16[4,256,8,64]{3,1,2,0:T(8,128)(2,1)S(1)}, bf16[4,256,8,64]{3,1,2,0:T(8,128)(2,1)S(1)}) fusion(f32[4,256,8,64]{3,1,2,0:T(8,128)} %copy.33, f32[4,256,8,64]{3,1,2,0:T(8,128)} %copy.32, f32[4,256,64]{2,1,0:T(8,128)S(1)} %get-tuple-element.22, f32[4,256,64]{2,1,0:T(8,128)S(1)} %get-tuple-element.21), kind=kLoop, calls=%fused_computation.3 | loop fusion | flops 4194304 | bytes 6815744 | tf_op jit(solution)/shard_map/convert.6
  31.8 0.0 copy-start.1
  31.8 1.3 select_reduce_fusion
  33.2 0.2 fusion.34
  33.4 0.0 copy-done.1
  33.4 0.6 copy.36
  34.0 0.4 fusion.30
  34.5 0.1 copy.27
  34.6 5.7 %collective-permute-start = (bf16[4,8,1024]{2,0,1:T(4,128)(2,1)S(1)}, bf16[4,8,1024]{2,0,1:T(4,128)(2,1)S(1)}, u32[]{:S(2)}, u32[]{:S(2)}) collective-permute-start(bf16[4,8,1024]{2,0,1:T(4,128)(2,1)S(1)} %copy.27), channel_id=1, source_target_pairs={{0,128},{1,129},{2,130},{3,131},{4,132},{5,133},{6,134},{7,135},{8... | collective-permute-start | bytes 196616 | tf_op jit(solution)/shard_map/ppermute | solution.py:19
  40.3 1.3 collective-permute-done
  41.6 15.3 %all_to_all.20 = bf16[4,8,1024]{2,0,1:T(4,128)(2,1)S(1)} all-to-all(bf16[4,8,1024]{2,0,1:T(4,128)(2,1)S(1)} %collective-permute-done), channel_id=1, replica_groups=mesh['side'=2,'row'=8,'col'=16] {'row'}, dimensions={1} | all-to-all | bytes 131072 | tf_op jit(solution)/shard_map/all_to_all | solution.py:103
  56.9 0.6 copy.28
  57.5 0.0 all-gather.3.cloned.1.call-update
  57.5 0.0 all-reduce.5.cloned.1.call-start
  57.6 34.6 %all-gather.3.cloned.1.call-done = bf16[8,64,1,1024]{3,0,2,1:T(8,128)(2,1)} async-done(((bf16[8,4,1,1024]{3,0,2,1:T(8,128)(2,1)}), bf16[8,64,1,1024]{3,0,2,1:T(8,128)(2,1)}) %all-gather.3.cloned.1.call-update) | async-done | bytes 1048592 | tf_op jit(solution)/shard_map/all_gather | solution.py:108
  92.2 1.8 copy.29
  94.0 0.0 copy-start.6
  94.0 0.0 copy-start.2
  94.1 2.8 convolution_convert_fusion.2
  96.9 0.0 all-reduce.5.cloned.1.call-update
  96.9 0.0 all-reduce.9.cloned.1.call-start
  96.9 0.0 copy-done.6
  96.9 68.6 %all-reduce.5.cloned.1.call-done = bf16[512,512]{1,0:T(8,128)(2,1)} async-done(((bf16[512,512]{1,0:T(8,128)(2,1)}), bf16[512,512]{1,0:T(8,128)(2,1)}) %all-reduce.5.cloned.1.call-update) | async-done | bytes 524304 | tf_op jit(solution)/shard_map/psum | solution.py:114
  165.5 0.0 copy-done.2
  165.5 1.3 multiply_reduce_fusion
  166.8 31.7 %psum.36 = f32[512]{0:T(512)S(1)} all-reduce(f32[512]{0:T(512)S(1)} %get-tuple-element.13), channel_id=1, replica_groups=mesh['side'=2,'row'=8,'col'=16] {'col'}, use_global_device_ids=true, to_apply=%region_4.5 | all-reduce | flops 512 | bytes 4096 | tf_op jit(solution)/shard_map/psum | solution.py:118
  198.6 0.0 copy-done
  198.6 0.0 copy-start.3
  198.6 0.0 copy-start.7
  198.6 3.6 convolution_convert_fusion.1
  202.2 0.0 copy-done.3
  202.2 0.0 copy-done.7
  202.2 2.5 convolution_convert_fusion
  204.7 0.0 all-reduce.9.cloned.1.call-update
  204.7 0.0 all-reduce.7.cloned.1.call-start
  204.8 129.6 %all-reduce.9.cloned.1.call-done = (bf16[512,1792]{1,0:T(8,128)(2,1)}, bf16[512,1792]{1,0:T(8,128)(2,1)}) async-done(((bf16[512,1792]{1,0:T(8,128)(2,1)}, bf16[512,1792]{1,0:T(8,128)(2,1)}), (bf16[512,1792]{1,0:T(8,128)(2,1)}, bf16[512,1792]{1,0:T(8,128)(2,1)})) %all-reduce.9.cloned.1.call-update) | async-done | bytes 3670032 | tf_op jit(solution)/shard_map/psum | solution.py:130
  334.4 4.6 %fusion.16 = bf16[512,512]{1,0:T(8,128)(2,1)} fusion(bf16[1,1792,512]{2,1,0:T(8,128)(2,1)} %param.21, bf16[512,1792]{1,0:T(8,128)(2,1)} %get-tuple-element.5, bf16[512,1792]{1,0:T(8,128)(2,1)} %get-tuple-element.6), kind=kOutput, calls=%fused_computation.21 | convolution fusion | flops 947126272 | bytes 6029312 | tf_op jit(solution)/shard_map/dot_general | solution.py:133
  339.0 0.0 all-reduce.7.cloned.1.call-update
  339.0 70.0 %all-reduce.7.cloned.1.call-done = bf16[512,512]{1,0:T(8,128)(2,1)} async-done(((bf16[512,512]{1,0:T(8,128)(2,1)}), bf16[512,512]{1,0:T(8,128)(2,1)}) %all-reduce.7.cloned.1.call-update) | async-done | bytes 524304 | tf_op jit(solution)/shard_map/psum | solution.py:134
  409.1 0.9 fusion.37
  410.1 16.1 %all_to_all.21 = bf16[16,4,512]{2,1,0:T(4,128)(2,1)S(1)} all-to-all(bf16[16,4,512]{2,1,0:T(4,128)(2,1)S(1)} %constant_dynamic-update-slice_fusion), channel_id=1, replica_groups=mesh['side'=2,'row'=8,'col'=16] {'col'}, dimensions={0} | all-to-all | bytes 131072 | tf_op jit(solution)/shard_map/all_to_all | solution.py:139
  426.2 1.3 collective-permute-start.1
  427.5 4.9 %collective-permute-done.1 = bf16[4,4096]{1,0:T(4,128)(2,1)S(1)} collective-permute-done((bf16[4,4096]{1,0:T(4,128)(2,1)S(1)}, bf16[4,4096]{1,0:T(4,128)(2,1)S(1)}, u32[]{:S(2)}, u32[]{:S(2)}) %collective-permute-start.1) | collective-permute-done | bytes 32800 | tf_op jit(solution)/shard_map/ppermute | solution.py:19
  432.4 0.6 slice_select_fusion
  (28 shorter events, 0.3 us)
Async XLA Ops:
  6.5 192.0 %copy-start = (bf16[1,512,1792]{2,1,0:T(8,128)(2,1)S(1)}, bf16[1,512,1792]{2,1,0:T(8,128)(2,1)}, u32[]{:S(2)}) copy-start(bf16[1,512,1792]{2,1,0:T(8,128)(2,1)} %param.19) | copy-start | bytes 5505028
  6.5 85.7 %all-gather.3.cloned.1.call-start = ((), (), s32[]{:S(2)}) async-start(), calls=%async_computation.4 | async-start | bytes 1114112 | tf_op jit(solution)/shard_map/all_gather | solution.py:108
  20.6 3.8 copy-start.4
  20.6 3.9 copy-start.5
  31.8 1.6 copy-start.1
  34.6 7.0 %collective-permute-start = (bf16[4,8,1024]{2,0,1:T(4,128)(2,1)S(1)}, bf16[4,8,1024]{2,0,1:T(4,128)(2,1)S(1)}, u32[]{:S(2)}, u32[]{:S(2)}) collective-permute-start(bf16[4,8,1024]{2,0,1:T(4,128)(2,1)S(1)} %copy.27), channel_id=1, source_target_pairs={{0,128},{1,129},{2,130},{3,131},{4,132},{5,133},{6,134},{7,135},{8... | collective-permute-start | bytes 196616 | tf_op jit(solution)/shard_map/ppermute | solution.py:19
  57.5 108.0 %all-reduce.5.cloned.1.call-start = ((), (), s32[]{:S(2)}) async-start(), calls=%async_computation.2 | async-start | bytes 1048576 | tf_op jit(solution)/shard_map/psum | solution.py:114
  94.0 2.9 copy-start.6
  94.0 71.5 %copy-start.2 = (bf16[512,512]{1,0:T(8,128)(2,1)S(1)}, bf16[512,512]{1,0:T(8,128)(2,1)}, u32[]{:S(2)}) copy-start(bf16[512,512]{1,0:T(8,128)(2,1)} %param.16) | copy-start | bytes 1572868
  96.9 237.5 %all-reduce.9.cloned.1.call-start = ((), (), s32[]{:S(2)}) async-start(), calls=%async_computation.5 | async-start | bytes 7340032 | tf_op jit(solution)/shard_map/psum | solution.py:130
  198.6 3.7 copy-start.3
  198.6 3.7 copy-start.7
  204.7 204.3 %all-reduce.7.cloned.1.call-start = ((), (), s32[]{:S(2)}) async-start(), calls=%async_computation.3 | async-start | bytes 1048576 | tf_op jit(solution)/shard_map/psum | solution.py:134
  426.2 6.2 %collective-permute-start.1 = (bf16[4,4096]{1,0:T(4,128)(2,1)S(1)}, bf16[4,4096]{1,0:T(4,128)(2,1)S(1)}, u32[]{:S(2)}, u32[]{:S(2)}) collective-permute-start(bf16[4,4096]{1,0:T(4,128)(2,1)S(1)} %slice.46), channel_id=1, source_target_pairs={{128,0},{129,1},{130,2},{131,3},{132,4},{133,5},{134,6},{135,7},{1... | collective-permute-start | bytes 98312 | tf_op jit(solution)/shard_map/ppermute | solution.py:19
Sparse Core Ops, SparseCore 0:
  57.7 34.5 all-gather.2
  97.0 68.4 all-reduce.4
  204.8 129.5 all-reduce.8
  339.1 69.8 all-reduce.6
